TPU v7x, 32 devices: a whole 2x2x4 slice. The times are simulated.
32 devices in a mesh: hid: 8 (over z, core), wid: 4 (over y, x).
Axes of the slice: x: 2, y: 2, z: 4, core: 2. Of those that a mesh axis runs over, the one named last changes fastest.
Arguments:
- grad_out: bfloat16 [64, 12288], P('hid', 'wid'), may hold values from -3 to 3
- pre_act: bfloat16 [64, 49152], P(None, 'hid'), may hold values from -6 to 6
- weight: bfloat16 [49152, 12288], P('hid', 'wid'), may hold values from -0.02734375 to 0.02734375
Outputs:
- grad_pre: bfloat16 [64, 49152], P('wid', 'hid')
- grad_weight: bfloat16 [49152, 12288], P('hid', 'wid')
All inputs are finite; a program needn't handle non-finite values.
Results may differ from a plain program's by a relative error of at most 0.0051.
Values may be sent and summed in bfloat16 or wider, within the bound.
No kernel may reach another device: no remote copies, remote signals or barrier semaphores. Data moves between devices by JAX's collectives and lax.ppermute only.
A program may use at most 128 MiB of HBM per device.

v0:
```python
import math
import jax
import jax.numpy as jnp
from jax import lax
from jax.sharding import PartitionSpec as P

coef = math.sqrt(2.0 / math.pi)


def gelu_parts(x):
    inner = coef * (x + 0.044715 * x * x * x)
    tangent = jnp.tanh(inner)
    value = 0.5 * x * (1.0 + tangent)
    slope = 0.5 * (1.0 + tangent) + 0.5 * x * (1.0 - tangent * tangent) * coef * (
        1.0 + 3.0 * 0.044715 * x * x
    )
    return (value, slope)


def contract_rows(left, right):
    return lax.dot_general(
        left, right, (((0,), (0,)), ((), ())), preferred_element_type=jnp.float32
    )


def contract_cols(left, right):
    return lax.dot_general(
        left, right, (((1,), (1,)), ((), ())), preferred_element_type=jnp.float32
    )


def local(grad_out, pre_act, weight):
    value, unused = gelu_parts(pre_act.astype(jnp.float32))
    hidden = value.astype(jnp.bfloat16)
    gathered = lax.all_gather(grad_out, "hid", axis=0, tiled=True)
    grad_w = contract_rows(hidden, gathered)
    partial_value = contract_cols(gathered, weight)
    share = lax.psum_scatter(partial_value, "wid", scatter_dimension=0, tiled=True)
    own_rows = share.shape[0]
    offset = lax.axis_index("wid") * own_rows
    local_pre = lax.dynamic_slice_in_dim(pre_act, offset, own_rows, 0)
    unused_value, slope = gelu_parts(local_pre.astype(jnp.float32))
    grad_pre = (share * slope).astype(jnp.bfloat16)
    return (grad_pre, grad_w.astype(jnp.bfloat16))


def solution(mesh):
    return jax.shard_map(
        local,
        mesh=mesh,
        in_specs=(P("hid", "wid"), P(None, "hid"), P("hid", "wid")),
        out_specs=(P("wid", "hid"), P("hid", "wid")),
        check_vma=False,
    )
```

profile of v0, /device:TPU:0, one launch (start us, length us, event | category | flops | bytes accessed | tf_op | source)
XLA Modules:
  0.0 83.0 jit_solution(14676352917141983411)
XLA Ops:
  7.2 0.0 reduce-scatter.2.cloned.1.call-start
  7.2 16.4 %all_gather.3 = bf16[64,3072]{1,0:T(8,128)(2,1)S(1)} all-gather(bf16[8,3072]{1,0:T(8,128)(2,1)} %param.3), channel_id=1, replica_groups=mesh['hid'=8,'wid'=4] {'hid'}, dimensions={0}, use_global_device_ids=true | all-gather | bytes 442368 | tf_op jit(solution)/shard_map/all_gather | solution.py:35
  23.7 18.2 %fusion.23 = f32[64,6144]{1,0:T(8,128)} fusion(bf16[64,3072]{1,0:T(8,128)(2,1)S(1)} %all_gather.3, bf16[6144,3072]{1,0:T(8,128)(2,1)} %param.5), kind=kOutput, calls=%fused_computation.35 | convolution fusion | flops 2415919104 | bytes 39714816 | tf_op jit(solution)/shard_map/dot_general | solution.py:27
  41.8 0.0 copy-start
  41.8 0.0 reduce-scatter.2.cloned.1.call-update
  41.9 1.1 %copy-done = bf16[64,6144]{1,0:T(8,128)(2,1)S(1)} copy-done((bf16[64,6144]{1,0:T(8,128)(2,1)S(1)}, bf16[64,6144]{1,0:T(8,128)(2,1)}, u32[]{:S(2)}) %copy-start) | copy-done | bytes 786456
  43.0 16.5 %convolution_convert_fusion = bf16[6144,3072]{1,0:T(8,128)(2,1)} fusion(bf16[64,3072]{1,0:T(8,128)(2,1)S(1)} %all_gather.3, bf16[64,6144]{1,0:T(8,128)(2,1)S(1)} %copy-done), kind=kOutput, calls=%fused_computation | convolution fusion | flops 2438725632 | bytes 38928384 | tf_op jit(solution)/shard_map/dot_general | solution.py:21
  59.5 14.7 %reduce-scatter.2.cloned.1.call-done = f32[16,6144]{1,0:T(8,128)} async-done(((f32[64,6144]{1,0:T(8,128)}), f32[16,6144]{1,0:T(8,128)}) %reduce-scatter.2.cloned.1.call-update) | async-done | bytes 393232 | tf_op jit(solution)/shard_map/reduce_scatter | solution.py:38
  74.2 1.9 %fusion.17 = bf16[16,6144]{1,0:T(8,128)(2,1)} fusion(f32[16,6144]{1,0:T(8,128)} %reduce-scatter.2.cloned.1.call-done, bf16[64,6144]{1,0:T(8,128)(2,1)S(1)} %copy-done, s32[]{:T(128)S(6)} %select_n.3), kind=kLoop, calls=%fused_computation.29 | loop fusion | flops 1966080 | bytes 786436 | tf_op jit(solution)/shard_map/convert_element_type | solution.py:43
Async XLA Ops:
  7.2 67.0 %reduce-scatter.2.cloned.1.call-start = ((), (), s32[]{:S(2)}) async-start(), calls=%async_computation.1 | async-start | bytes 1966080 | tf_op jit(solution)/shard_map/reduce_scatter | solution.py:38
  41.8 1.1 %copy-start = (bf16[64,6144]{1,0:T(8,128)(2,1)S(1)}, bf16[64,6144]{1,0:T(8,128)(2,1)}, u32[]{:S(2)}) copy-start(bf16[64,6144]{1,0:T(8,128)(2,1)} %param.4) | copy-start | bytes 2359300
Sparse Core Ops, SparseCore 0:
  42.0 32.1 reduce-scatter.1
where the time goes:
time: 83.2 us; the launch traced here: 83 us
  matrix products  34.7 us (42%)
  blocking collectives  16.4 us (20%)
  waiting for transfers between devices  14.7 us (18%)
  between operations  14 us (17%)
  other arithmetic  1.94 us (2%)
  local copies, waits for them, and re-layouts  1.1 us (1%)
    dot_general x1, matrix products, contract_cols(): lax.dot_general(left, right, (((1,), (1,)), ((), ())), preferred_element_...  18.2 us
    dot_general x1, matrix products, contract_rows(): lax.dot_general(left, right, (((0,), (0,)), ((), ())), preferred_element_...  16.5 us
    all_gather x1, blocking collectives, local(): gathered = lax.all_gather(grad_out, 'hid', axis=0, tiled=True)  16.4 us
    reduce_scatter x1, waiting for transfers between devices, local(): lax.psum_scatter(partial_value, 'wid', scatter_dimension=0, tiled=True)  14.7 us
    convert_element_type x1, other arithmetic, local(): grad_pre = (share * slope).astype(jnp.bfloat16)  1.94 us
  transfers between devices with their start and end apart: 1, of which 1 were waited for; matrix products, arithmetic and copies ran while one was open for 20% of the time, Pallas kernels for 0%

commit v1 on v0

--- a/solution.py
+++ b/solution.py
@@ -32,7 +32,21 @@
 def local(grad_out, pre_act, weight):
     value, unused = gelu_parts(pre_act.astype(jnp.float32))
     hidden = value.astype(jnp.bfloat16)
-    gathered = lax.all_gather(grad_out, "hid", axis=0, tiled=True)
+    ways, here, step = (lax.axis_size("hid"), lax.axis_index("hid"), grad_out.shape[0])
+    dims = [n * ways if d == 0 else n for d, n in enumerate(grad_out.shape)]
+    full = lax.dynamic_update_slice_in_dim(
+        jnp.zeros(dims, grad_out.dtype), grad_out, here * step, axis=0
+    )
+    going_up = going_down = grad_out
+    for far in range(1, ways // 2 + 1):
+        going_up = lax.ppermute(going_up, "hid", [(d, (d + 1) % ways) for d in range(ways)])
+        full = lax.dynamic_update_slice_in_dim(full, going_up, (here - far) % ways * step, axis=0)
+        if 2 * far < ways:
+            going_down = lax.ppermute(going_down, "hid", [(d, (d - 1) % ways) for d in range(ways)])
+            full = lax.dynamic_update_slice_in_dim(
+                full, going_down, (here + far) % ways * step, axis=0
+            )
+    gathered = full
     grad_w = contract_rows(hidden, gathered)
     partial_value = contract_cols(gathered, weight)
     share = lax.psum_scatter(partial_value, "wid", scatter_dimension=0, tiled=True)

time: 83.2 us -> 90.1 us (1.083)
  blocking collectives: 16.4 us -> 0 us
  starting transfers between devices: 0.04 us -> 11.7 us
  waiting for transfers between devices: 14.7 us -> 25.4 us
  local copies, waits for them, and re-layouts: 1.1 us -> 2.03 us
    all_gather x1 -> x0, blocking collectives: 16.4 us -> none  [local(): gathered = lax.all_gather(grad_out, 'hid', axis=0, tiled=True)]
    ppermute x0 -> x7, waiting for transfers between devices: none -> 13.5 us  [the longest x4 10.6 us: local(): lax.ppermute(going_up, 'hid', [(d, (d + 1) % ways) for d in range(ways)])]
    ppermute x0 -> x7, starting transfers between devices: none -> 11.6 us  [the longest x3 11.6 us: local(): lax.ppermute(going_down, 'hid', [(d, (d - 1) % ways) for d in range(ways)])]
    reduce_scatter x1, waiting for transfers between devices: 14.7 us -> 11.9 us  [local(): lax.psum_scatter(partial_value, 'wid', scatter_dimension=0, tiled=True)]
  transfers between devices with their start and end apart: 1 -> 8, of which waited for: 1 -> 5; matrix products, arithmetic and copies ran while one was open for 20% -> 19% of each run, Pallas kernels for 0% -> 0%
where the time goes in v1:
time: 90.1 us; the launch traced here: 89.8 us
  matrix products  34.7 us (39%)
  waiting for transfers between devices  25.4 us (28%)
  between operations  14.1 us (16%)
  starting transfers between devices  11.7 us (13%)
  local copies, waits for them, and re-layouts  2.03 us (2%)
  other arithmetic  1.94 us (2%)
    dot_general x1, matrix products, contract_cols(): lax.dot_general(left, right, (((1,), (1,)), ((), ())), preferred_element_...  18.2 us
    dot_general x1, matrix products, contract_rows(): lax.dot_general(left, right, (((0,), (0,)), ((), ())), preferred_element_...  16.5 us
    reduce_scatter x1, waiting for transfers between devices, local(): lax.psum_scatter(partial_value, 'wid', scatter_dimension=0, tiled=True)  11.9 us
    ppermute x3, starting transfers between devices, local(): lax.ppermute(going_down, 'hid', [(d, (d - 1) % ways) for d in range(ways)])  11.6 us
    ppermute x4, waiting for transfers between devices, local(): lax.ppermute(going_up, 'hid', [(d, (d + 1) % ways) for d in range(ways)])  10.6 us
    ppermute x3, waiting for transfers between devices, local(): lax.ppermute(going_down, 'hid', [(d, (d - 1) % ways) for d in range(ways)])  2.86 us
    convert_element_type x1, other arithmetic, local(): grad_pre = (share * slope).astype(jnp.bfloat16)  1.94 us
  transfers between devices with their start and end apart: 8, of which 5 were waited for; matrix products, arithmetic and copies ran while one was open for 19% of the time, Pallas kernels for 0%

profile of v1, /device:TPU:0, one launch (start us, length us, event | category | flops | bytes accessed | tf_op | source)
XLA Modules:
  0.0 89.8 jit_solution(17211316341070625891)
XLA Ops:
  7.2 0.0 reduce-scatter.2.cloned.1.call-start
  7.2 4.6 %collective-permute-start.1 = (bf16[8,3072]{1,0:T(8,128)(2,1)}, bf16[8,3072]{1,0:T(8,128)(2,1)S(1)}, u32[]{:S(2)}, u32[]{:S(2)}) collective-permute-start(bf16[8,3072]{1,0:T(8,128)(2,1)} %param.3), channel_id=1, source_target_pairs={{0,28},{4,0},{8,4},{12,8},{16,12},{20,16},{24,20},{28,24},{1,29},{... | collective-permute-start | bytes 147464 | tf_op jit(solution)/shard_map/ppermute | solution.py:45
  11.8 0.0 collective-permute-start
  11.8 0.8 constant_dynamic-update-slice_fusion.7
  12.7 1.2 %collective-permute-done.1 = bf16[8,3072]{1,0:T(8,128)(2,1)S(1)} collective-permute-done((bf16[8,3072]{1,0:T(8,128)(2,1)}, bf16[8,3072]{1,0:T(8,128)(2,1)S(1)}, u32[]{:S(2)}, u32[]{:S(2)}) %collective-permute-start.1) | collective-permute-done | bytes 49184 | tf_op jit(solution)/shard_map/ppermute | solution.py:45
  13.8 3.5 %collective-permute-start.3 = (bf16[8,3072]{1,0:T(8,128)(2,1)S(1)}, bf16[8,3072]{1,0:T(8,128)(2,1)S(1)}, u32[]{:S(2)}, u32[]{:S(2)}) collective-permute-start(bf16[8,3072]{1,0:T(8,128)(2,1)S(1)} %collective-permute-done.1), channel_id=1, source_target_pairs={{0,28},{4,0},{8,4},{12,8},{16,12},{20,16},{24,20},{28,24},{1,29},{... | collective-permute-start | bytes 147464 | tf_op jit(solution)/shard_map/ppermute | solution.py:45
  17.3 0.0 collective-permute-done
  17.4 0.0 collective-permute-start.2
  17.4 1.7 %collective-permute-done.3 = bf16[8,3072]{1,0:T(8,128)(2,1)S(1)} collective-permute-done((bf16[8,3072]{1,0:T(8,128)(2,1)S(1)}, bf16[8,3072]{1,0:T(8,128)(2,1)S(1)}, u32[]{:S(2)}, u32[]{:S(2)}) %collective-permute-start.3) | collective-permute-done | bytes 49184 | tf_op jit(solution)/shard_map/ppermute | solution.py:45
  19.1 3.6 %collective-permute-start.5 = (bf16[8,3072]{1,0:T(8,128)(2,1)S(1)}, bf16[8,3072]{1,0:T(8,128)(2,1)S(1)}, u32[]{:S(2)}, u32[]{:S(2)}) collective-permute-start(bf16[8,3072]{1,0:T(8,128)(2,1)S(1)} %collective-permute-done.3), channel_id=1, source_target_pairs={{0,28},{4,0},{8,4},{12,8},{16,12},{20,16},{24,20},{28,24},{1,29},{... | collective-permute-start | bytes 147464 | tf_op jit(solution)/shard_map/ppermute | solution.py:45
  22.6 0.0 collective-permute-done.2
  22.7 0.0 collective-permute-start.4
  22.7 5.3 %collective-permute-done.4 = bf16[8,3072]{1,0:T(8,128)(2,1)S(1)} collective-permute-done((bf16[8,3072]{1,0:T(8,128)(2,1)S(1)}, bf16[8,3072]{1,0:T(8,128)(2,1)S(1)}, u32[]{:S(2)}, u32[]{:S(2)}) %collective-permute-start.4) | collective-permute-done | bytes 49184 | tf_op jit(solution)/shard_map/ppermute | solution.py:42
  28.0 0.0 collective-permute-start.6
  28.0 0.0 collective-permute-done.5
  28.0 5.3 %collective-permute-done.6 = bf16[8,3072]{1,0:T(8,128)(2,1)S(1)} collective-permute-done((bf16[8,3072]{1,0:T(8,128)(2,1)S(1)}, bf16[8,3072]{1,0:T(8,128)(2,1)S(1)}, u32[]{:S(2)}, u32[]{:S(2)}) %collective-permute-start.6) | collective-permute-done | bytes 49184 | tf_op jit(solution)/shard_map/ppermute | solution.py:42
  33.3 18.2 %fusion.23 = f32[64,6144]{1,0:T(8,128)} fusion(bf16[64,3072]{1,0:T(8,128)(2,1)S(1)} %constant_dynamic-update-slice_fusion, bf16[6144,3072]{1,0:T(8,128)(2,1)} %param.5), kind=kOutput, calls=%fused_computation.43 | convolution fusion | flops 2415919104 | bytes 39714816 | tf_op jit(solution)/shard_map/dot_general | solution.py:27
  51.5 0.0 copy-start
  51.5 0.0 reduce-scatter.2.cloned.1.call-update
  51.5 1.1 %copy-done = bf16[64,6144]{1,0:T(8,128)(2,1)S(1)} copy-done((bf16[64,6144]{1,0:T(8,128)(2,1)S(1)}, bf16[64,6144]{1,0:T(8,128)(2,1)}, u32[]{:S(2)}) %copy-start) | copy-done | bytes 786456
  52.6 16.5 %convolution_convert_fusion = bf16[6144,3072]{1,0:T(8,128)(2,1)} fusion(bf16[64,3072]{1,0:T(8,128)(2,1)S(1)} %constant_dynamic-update-slice_fusion, bf16[64,6144]{1,0:T(8,128)(2,1)S(1)} %copy-done), kind=kOutput, calls=%fused_computation | convolution fusion | flops 2438725632 | bytes 38928384 | tf_op jit(solution)/shard_map/dot_general | solution.py:21
  69.1 11.9 %reduce-scatter.2.cloned.1.call-done = f32[16,6144]{1,0:T(8,128)} async-done(((f32[64,6144]{1,0:T(8,128)}), f32[16,6144]{1,0:T(8,128)}) %reduce-scatter.2.cloned.1.call-update) | async-done | bytes 393232 | tf_op jit(solution)/shard_map/reduce_scatter | solution.py:52
  81.0 1.9 %fusion.17 = bf16[16,6144]{1,0:T(8,128)(2,1)} fusion(f32[16,6144]{1,0:T(8,128)} %reduce-scatter.2.cloned.1.call-done, bf16[64,6144]{1,0:T(8,128)(2,1)S(1)} %copy-done, s32[]{:T(128)S(6)} %select_n.73), kind=kLoop, calls=%fused_computation.29 | loop fusion | flops 1966080 | bytes 786436 | tf_op jit(solution)/shard_map/convert_element_type | solution.py:57
  (8 shorter events, 0.1 us)
Async XLA Ops:
  7.2 73.8 %reduce-scatter.2.cloned.1.call-start = ((), (), s32[]{:S(2)}) async-start(), calls=%async_computation.1 | async-start | bytes 1966080 | tf_op jit(solution)/shard_map/reduce_scatter | solution.py:52
  7.2 6.6 %collective-permute-start.1 = (bf16[8,3072]{1,0:T(8,128)(2,1)}, bf16[8,3072]{1,0:T(8,128)(2,1)S(1)}, u32[]{:S(2)}, u32[]{:S(2)}) collective-permute-start(bf16[8,3072]{1,0:T(8,128)(2,1)} %param.3), channel_id=1, source_target_pairs={{0,28},{4,0},{8,4},{12,8},{16,12},{20,16},{24,20},{28,24},{1,29},{... | collective-permute-start | bytes 147464 | tf_op jit(solution)/shard_map/ppermute | solution.py:45
  11.8 5.6 %collective-permute-start = (bf16[8,3072]{1,0:T(8,128)(2,1)}, bf16[8,3072]{1,0:T(8,128)(2,1)S(1)}, u32[]{:S(2)}, u32[]{:S(2)}) collective-permute-start(bf16[8,3072]{1,0:T(8,128)(2,1)} %param.3), channel_id=1, source_target_pairs={{0,4},{4,8},{8,12},{12,16},{16,20},{20,24},{24,28},{28,0},{1,5},{5... | collective-permute-start | bytes 147464 | tf_op jit(solution)/shard_map/ppermute | solution.py:42
  13.8 5.2 %collective-permute-start.3 = (bf16[8,3072]{1,0:T(8,128)(2,1)S(1)}, bf16[8,3072]{1,0:T(8,128)(2,1)S(1)}, u32[]{:S(2)}, u32[]{:S(2)}) collective-permute-start(bf16[8,3072]{1,0:T(8,128)(2,1)S(1)} %collective-permute-done.1), channel_id=1, source_target_pairs={{0,28},{4,0},{8,4},{12,8},{16,12},{20,16},{24,20},{28,24},{1,29},{... | collective-permute-start | bytes 147464 | tf_op jit(solution)/shard_map/ppermute | solution.py:45
  17.4 5.3 %collective-permute-start.2 = (bf16[8,3072]{1,0:T(8,128)(2,1)S(1)}, bf16[8,3072]{1,0:T(8,128)(2,1)S(1)}, u32[]{:S(2)}, u32[]{:S(2)}) collective-permute-start(bf16[8,3072]{1,0:T(8,128)(2,1)S(1)} %collective-permute-done), channel_id=1, source_target_pairs={{0,4},{4,8},{8,12},{12,16},{16,20},{20,24},{24,28},{28,0},{1,5},{5... | collective-permute-start | bytes 147464 | tf_op jit(solution)/shard_map/ppermute | solution.py:42
  19.1 8.9 %collective-permute-start.5 = (bf16[8,3072]{1,0:T(8,128)(2,1)S(1)}, bf16[8,3072]{1,0:T(8,128)(2,1)S(1)}, u32[]{:S(2)}, u32[]{:S(2)}) collective-permute-start(bf16[8,3072]{1,0:T(8,128)(2,1)S(1)} %collective-permute-done.3), channel_id=1, source_target_pairs={{0,28},{4,0},{8,4},{12,8},{16,12},{20,16},{24,20},{28,24},{1,29},{... | collective-permute-start | bytes 147464 | tf_op jit(solution)/shard_map/ppermute | solution.py:45
  22.7 5.3 %collective-permute-start.4 = (bf16[8,3072]{1,0:T(8,128)(2,1)S(1)}, bf16[8,3072]{1,0:T(8,128)(2,1)S(1)}, u32[]{:S(2)}, u32[]{:S(2)}) collective-permute-start(bf16[8,3072]{1,0:T(8,128)(2,1)S(1)} %collective-permute-done.2), channel_id=1, source_target_pairs={{0,4},{4,8},{8,12},{12,16},{16,20},{20,24},{24,28},{28,0},{1,5},{5... | collective-permute-start | bytes 147464 | tf_op jit(solution)/shard_map/ppermute | solution.py:42
  28.0 5.3 %collective-permute-start.6 = (bf16[8,3072]{1,0:T(8,128)(2,1)S(1)}, bf16[8,3072]{1,0:T(8,128)(2,1)S(1)}, u32[]{:S(2)}, u32[]{:S(2)}) collective-permute-start(bf16[8,3072]{1,0:T(8,128)(2,1)S(1)} %collective-permute-done.4), channel_id=1, source_target_pairs={{0,4},{4,8},{8,12},{12,16},{16,20},{20,24},{24,28},{28,0},{1,5},{5... | collective-permute-start | bytes 147464 | tf_op jit(solution)/shard_map/ppermute | solution.py:42
  51.5 1.1 %copy-start = (bf16[64,6144]{1,0:T(8,128)(2,1)S(1)}, bf16[64,6144]{1,0:T(8,128)(2,1)}, u32[]{:S(2)}) copy-start(bf16[64,6144]{1,0:T(8,128)(2,1)} %param.4) | copy-start | bytes 2359300
Sparse Core Ops, SparseCore 0:
  51.6 29.3 reduce-scatter.1
